TPU v7x, 512 devices: a whole 4x8x8 slice. The times are simulated.
512 devices in a mesh: tok: 64 (over z, y), tp: 8 (over x, core).
Axes of the slice: x: 4, y: 8, z: 8, core: 2. Of those that a mesh axis runs over, the one named last changes fastest.
Arguments:
- activations: bfloat16 [8192, 4096], P('tok', 'tp'), may hold values from -6 to 6
- out_grad: bfloat16 [8192, 4096], P('tok', 'tp'), may hold values from -6 to 6
- routes: int32 [8192, 2], P('tok'), may hold values from 0 to 63, all different within a row; in each aligned block of 128 rows (0 to 127, 128 to 255, ...) at most 8 rows name the same one
- gate_vals: float32 [8192, 2], P('tok'), may hold values from 0.2 to 1
- w_gate: bfloat16 [64, 1536, 4096], P('tok', 'tp'), may hold values from -0.09375 to 0.09375
- w_up: bfloat16 [64, 1536, 4096], P('tok', 'tp'), may hold values from -0.09375 to 0.09375
- w_down: bfloat16 [64, 1536, 4096], P('tok', 'tp'), may hold values from -0.15625 to 0.15625
Outputs:
- in_grad: bfloat16 [8192, 4096], P('tok', 'tp')
Inputs may be any that keep to these rules, and one draw needn't show every extreme that they name: `routes`: each row names 2 different experts. In each aligned block of 128 rows (the tokens of one index of tok) no expert is named by more than 8 rows, a bound that some block reaches.
All inputs are finite; a program needn't handle non-finite values.
Results may differ from a plain program's by a relative error of at most 0.0057.
Values may be sent and summed in bfloat16 or wider, within the bound.
No kernel may reach another device: no remote copies, remote signals or barrier semaphores. Data moves between devices by JAX's collectives and lax.ppermute only.
A program may use at most 64 MiB of HBM per device.

v0:
```python
import jax
import jax.numpy as jnp
from jax import lax
from jax.sharding import PartitionSpec as P


def routing(routes, n_tok, capacity):
    tok_dev = routes.shape[0]
    top_k = routes.shape[1]
    flat = routes.reshape(-1)
    onehot = (flat[:, None] == jnp.arange(n_tok, dtype=jnp.int32)[None, :]).astype(jnp.int32)
    before = jnp.cumsum(onehot, axis=0) - onehot
    slot = jnp.sum(before * onehot, axis=1)
    position = flat * capacity + slot
    slot_count = n_tok * capacity
    hits = (position[:, None] == jnp.arange(slot_count, dtype=jnp.int32)[None, :]).astype(jnp.int32)
    hits = jnp.sum(hits.reshape(tok_dev, top_k, slot_count), axis=1)
    token_of = jnp.sum(hits * jnp.arange(tok_dev, dtype=jnp.int32)[:, None], axis=0)
    filled = jnp.sum(hits, axis=0) > 0
    return (position, token_of, filled)


def bucket(rows, token_of, filled):
    return jnp.where(filled[:, None], jnp.take(rows, token_of, axis=0), jnp.zeros((), rows.dtype))


def combine(returned, position, gate_vals):
    picked = jnp.take(returned, position, axis=0).reshape(
        gate_vals.shape[0], gate_vals.shape[1], returned.shape[1]
    )
    total = jnp.zeros((picked.shape[0], picked.shape[2]), jnp.float32)
    for column in range(gate_vals.shape[1]):
        total = total + gate_vals[:, column : column + 1] * picked[:, column].astype(jnp.float32)
    return total


def hidden_grads(gate_pre, up_pre, hidden_grad):
    sigma = jax.nn.sigmoid(gate_pre)
    silu_value = gate_pre * sigma
    slope = sigma * (1.0 + gate_pre * (1.0 - sigma))
    return (
        (hidden_grad * up_pre * slope).astype(jnp.bfloat16),
        (hidden_grad * silu_value).astype(jnp.bfloat16),
    )


def shards(activations, out_grad, routes, gate_vals, w_gate, w_up, w_down):
    n_tok = lax.axis_size("tok")
    tok_dev = routes.shape[0]
    top_k = routes.shape[1]
    capacity = max(2, 2 * tok_dev * top_k // n_tok)
    slot_count = n_tok * capacity
    gate_local = w_gate[0]
    up_local = w_up[0]
    down_local = w_down[0]
    contract_last = (((1,), (1,)), ((), ()))
    position, token_of, filled = routing(routes, n_tok, capacity)
    whole_x, whole_g = (
        lax.all_gather(activations, "tp", axis=1, tiled=True),
        lax.all_gather(out_grad, "tp", axis=1, tiled=True),
    )
    width = whole_x.shape[1]
    send_x = bucket(whole_x, token_of, filled).reshape(n_tok, capacity, width)
    send_g = bucket(whole_g, token_of, filled).reshape(n_tok, capacity, width)
    recv_x, recv_g = (
        lax.all_to_all(send_x, "tok", split_axis=0, concat_axis=0, tiled=True),
        lax.all_to_all(send_g, "tok", split_axis=0, concat_axis=0, tiled=True),
    )
    recv_x = recv_x.reshape(slot_count, width)
    recv_g = recv_g.reshape(slot_count, width)
    gate_pre = lax.dot_general(
        recv_x, gate_local, contract_last, preferred_element_type=jnp.float32
    )
    up_pre = lax.dot_general(recv_x, up_local, contract_last, preferred_element_type=jnp.float32)
    hidden_grad = lax.dot_general(
        recv_g, down_local, contract_last, preferred_element_type=jnp.float32
    )
    gate_grad, up_grad = hidden_grads(gate_pre, up_pre, hidden_grad)
    partial_value = jnp.dot(gate_grad, gate_local, preferred_element_type=jnp.float32)
    partial_value = partial_value + jnp.dot(up_grad, up_local, preferred_element_type=jnp.float32)
    partial_bf = partial_value.astype(jnp.bfloat16)
    full_width = partial_bf.shape[1]
    returned = lax.all_to_all(
        partial_bf.reshape(n_tok, capacity, full_width),
        "tok",
        split_axis=0,
        concat_axis=0,
        tiled=True,
    )
    combined = combine(returned.reshape(slot_count, full_width), position, gate_vals)
    summed = lax.psum_scatter(combined, "tp", scatter_dimension=1, tiled=True)
    return summed.astype(jnp.bfloat16)


def solution(mesh):
    placed = (
        P("tok", "tp"),
        P("tok", "tp"),
        P("tok", None),
        P("tok", None),
        P("tok", "tp", None),
        P("tok", "tp", None),
        P("tok", "tp", None),
    )
    return jax.shard_map(
        shards, mesh=mesh, in_specs=placed, out_specs=P("tok", "tp"), check_vma=False
    )
```

profile of v0, /device:TPU:16, one launch (start us, length us, event | category | flops | bytes accessed | tf_op | source)
XLA Modules:
  0.0 566.2 jit_solution(14401200045992333486)
XLA Ops:
  6.5 0.0 copy-start
  6.5 0.0 all-gather.3.cloned.1.call-start
  6.5 0.7 all-gather.3.cloned.1.call-update
  7.3 0.0 all-gather.5.cloned.1.call-start
  7.3 0.7 all-gather.5.cloned.1.call-update
  8.0 0.8 copy.23
  8.8 0.1 eq.40
  8.9 0.1 reshape.106
  9.1 0.6 reduce-window.6
  9.7 0.2 slice_reduce_fusion
  9.9 0.1 fusion.43
  10.0 0.1 reduce_sum.41
  10.2 0.1 copy.26
  10.3 0.7 compare_and_fusion.1
  11.0 0.1 convert_reduce_fusion.1
  11.2 31.5 %all-gather.3.cloned.1.call-done = bf16[128,4096]{1,0:T(8,128)(2,1)} async-done(((bf16[128,512]{1,0:T(8,128)(2,1)}), bf16[128,4096]{1,0:T(8,128)(2,1)}) %all-gather.3.cloned.1.call-update) | async-done | bytes 1048592 | tf_op jit(solution)/shard_map/all_gather | solution.py:60
  42.7 9.9 %gather_fusion.1 = bf16[512,4096]{1,0:T(8,128)(2,1)} fusion(bf16[128,4096]{1,0:T(8,128)(2,1)} %all-gather.3.cloned.1.call-done, s32[1024]{0:T(1024)S(1)} %pad_clamp_fusion.1), kind=kCustom, calls=%fused_computation.clone | custom fusion | bytes 8390656 | tf_op jit(solution)/shard_map/jit(_take)/gather | solution.py:24
  52.6 20.9 %all-gather.5.cloned.1.call-done = bf16[128,4096]{1,0:T(8,128)(2,1)} async-done(((bf16[128,512]{1,0:T(8,128)(2,1)}), bf16[128,4096]{1,0:T(8,128)(2,1)}) %all-gather.5.cloned.1.call-update) | async-done | bytes 1048592 | tf_op jit(solution)/shard_map/all_gather | solution.py:59
  73.5 9.9 %gather_fusion.2 = bf16[512,4096]{1,0:T(8,128)(2,1)} fusion(bf16[128,4096]{1,0:T(8,128)(2,1)} %all-gather.5.cloned.1.call-done, s32[1024]{0:T(1024)S(1)} %pad_clamp_fusion.1), kind=kCustom, calls=%fused_computation.1.clone | custom fusion | bytes 8390656 | tf_op jit(solution)/shard_map/jit(_take)/gather | solution.py:24
  83.4 5.4 fusion.7
  88.8 109.8 %all_to_all.15 = bf16[64,8,4096]{2,1,0:T(8,128)(2,1)} all-to-all(bf16[64,8,4096]{2,1,0:T(8,128)(2,1)S(1)} %get-tuple-element.12), channel_id=1, replica_groups=mesh['tok'=64,'tp'=8] {'tok'}, dimensions={0} | all-to-all | bytes 8388608 | tf_op jit(solution)/shard_map/all_to_all | solution.py:66
  198.5 0.0 copy-start.1
  198.5 16.3 %all-to-all-start = ((bf16[64,8,4096]{2,1,0:T(8,128)(2,1)}), bf16[64,8,4096]{2,1,0:T(8,128)(2,1)}, u32[]{:S(2)}, u32[]{:S(2)}) async-start(bf16[64,8,4096]{2,1,0:T(8,128)(2,1)} %get-tuple-element.13), calls=%async_computation | async-start | bytes 8388608 | tf_op jit(solution)/shard_map/all_to_all | solution.py:67
  214.9 0.0 copy-done.1
  214.9 3.7 fusion.1
  218.6 114.2 %all-to-all-done = bf16[64,8,4096]{2,1,0:T(8,128)(2,1)} async-done(((bf16[64,8,4096]{2,1,0:T(8,128)(2,1)}), bf16[64,8,4096]{2,1,0:T(8,128)(2,1)}, u32[]{:S(2)}, u32[]{:S(2)}) %all-to-all-start) | async-done | bytes 4194336 | tf_op jit(solution)/shard_map/all_to_all | solution.py:67
  332.8 5.0 fusion.5
  337.8 0.0 copy-done
  337.8 8.3 %fusion.10 = f32[512,4096]{1,0:T(8,128)} fusion(bf16[1,192,4096]{2,1,0:T(8,128)(2,1)S(1)} %copy-done.1, f32[512,192]{0,1:T(8,128)} %fusion.5, bf16[1,192,4096]{2,1,0:T(8,128)(2,1)S(1)} %copy-done, bf16[64,8,4096]{2,1,0:T(8,128)(2,1)} %all_to_all.15, f32[512,192]{0,1:T(8,128)S(1)} %fusion.1), kind=kOutput, calls=%fused_computation.19 | convolution fusion | flops 1611595776 | bytes 16515072 | tf_op jit(solution)/shard_map/dot_general | solution.py:79
  346.1 6.8 %fusion = bf16[64,8,4096]{2,1,0:T(8,128)(2,1)} fusion(f32[512,4096]{1,0:T(8,128)} %fusion.10, bf16[1,192,4096]{2,1,0:T(8,128)(2,1)S(1)} %copy-done, f32[512,192]{0,1:T(8,128)} %fusion.5, f32[512,192]{0,1:T(8,128)S(1)} %fusion.1), kind=kOutput, calls=%fused_computation.4 | convolution fusion | flops 810090496 | bytes 14942208 | tf_op jit(solution)/shard_map/dot_general | solution.py:80
  353.0 0.0 copy-start.2
  353.0 0.0 copy-start.3
  353.0 15.8 %all-to-all-start.2 = ((bf16[64,8,4096]{2,1,0:T(8,128)(2,1)}), bf16[64,8,4096]{2,1,0:T(8,128)(2,1)}, u32[]{:S(2)}, u32[]{:S(2)}) async-start(bf16[64,8,4096]{2,1,0:T(8,128)(2,1)} %fusion), calls=%async_computation.2 | async-start | bytes 8388608 | tf_op jit(solution)/shard_map/all_to_all | solution.py:83
  368.8 0.3 reduce-scatter.2.cloned.1.call-start
  369.1 0.0 copy-done.2
  369.1 0.1 copy.27
  369.2 0.1 mul.84
  369.4 0.0 copy-done.3
  369.4 110.9 %all-to-all-done.2 = bf16[64,8,4096]{2,1,0:T(8,128)(2,1)} async-done(((bf16[64,8,4096]{2,1,0:T(8,128)(2,1)}), bf16[64,8,4096]{2,1,0:T(8,128)(2,1)}, u32[]{:S(2)}, u32[]{:S(2)}) %all-to-all-start.2) | async-done | bytes 4194336 | tf_op jit(solution)/shard_map/all_to_all | solution.py:83
  480.3 7.9 %gather_fusion = bf16[256,4096]{1,0:T(8,128)(2,1)} fusion(bf16[512,4096]{1,0:T(8,128)(2,1)} %bitcast.10, s32[1024]{0:T(1024)S(1)} %pad_clamp_fusion), kind=kCustom, calls=%fused_computation.2 | custom fusion | bytes 4195328 | tf_op jit(solution)/shard_map/jit(_take)/gather | solution.py:28
  488.3 4.4 gather.10
  492.7 4.0 copy_select_fusion
  496.7 1.8 fusion.9
  498.5 0.0 reduce-scatter.2.cloned.1.call-update
  498.5 59.6 %reduce-scatter.2.cloned.1.call-done = f32[128,512]{1,0:T(8,128)} async-done(((f32[128,4096]{1,0:T(8,128)}), f32[128,512]{1,0:T(8,128)}) %reduce-scatter.2.cloned.1.call-update) | async-done | bytes 262160 | tf_op jit(solution)/shard_map/reduce_scatter | solution.py:91
  558.1 1.6 convert_element_type.45
  (11 shorter events, 0.1 us)
Async XLA Ops:
  6.5 331.3 %copy-start = (bf16[1,192,4096]{2,1,0:T(8,128)(2,1)S(1)}, bf16[1,192,4096]{2,1,0:T(8,128)(2,1)}, u32[]{:S(2)}) copy-start(bf16[1,192,4096]{2,1,0:T(8,128)(2,1)} %param.14) | copy-start | bytes 4718596
  6.5 36.1 %all-gather.3.cloned.1.call-start = ((), (), s32[]{:S(2)}) async-start(), calls=%async_computation.4 | async-start | bytes 1179648 | tf_op jit(solution)/shard_map/all_gather | solution.py:60
  7.3 66.2 %all-gather.5.cloned.1.call-start = ((), (), s32[]{:S(2)}) async-start(), calls=%async_computation.5 | async-start | bytes 1179648 | tf_op jit(solution)/shard_map/all_gather | solution.py:59
  198.5 16.4 %copy-start.1 = (bf16[1,192,4096]{2,1,0:T(8,128)(2,1)S(1)}, bf16[1,192,4096]{2,1,0:T(8,128)(2,1)}, u32[]{:S(2)}) copy-start(bf16[1,192,4096]{2,1,0:T(8,128)(2,1)} %param.13) | copy-start | bytes 4718596
  198.5 134.3 %all-to-all-start = ((bf16[64,8,4096]{2,1,0:T(8,128)(2,1)}), bf16[64,8,4096]{2,1,0:T(8,128)(2,1)}, u32[]{:S(2)}, u32[]{:S(2)}) async-start(bf16[64,8,4096]{2,1,0:T(8,128)(2,1)} %get-tuple-element.13), calls=%async_computation | async-start | bytes 8388608 | tf_op jit(solution)/shard_map/all_to_all | solution.py:67
  353.0 16.1 %copy-start.2 = (s32[128,2]{0,1:T(2,128)S(1)}, s32[128,2]{0,1:T(2,128)}, u32[]{:S(2)}) copy-start(s32[128,2]{0,1:T(2,128)} %param.11) | copy-start | bytes 3076
  353.0 16.4 %copy-start.3 = (f32[128,2]{0,1:T(2,128)S(1)}, f32[128,2]{0,1:T(2,128)}, u32[]{:S(2)}) copy-start(f32[128,2]{0,1:T(2,128)} %param.12) | copy-start | bytes 3076
  353.0 127.4 %all-to-all-start.2 = ((bf16[64,8,4096]{2,1,0:T(8,128)(2,1)}), bf16[64,8,4096]{2,1,0:T(8,128)(2,1)}, u32[]{:S(2)}, u32[]{:S(2)}) async-start(bf16[64,8,4096]{2,1,0:T(8,128)(2,1)} %fusion), calls=%async_computation.2 | async-start | bytes 8388608 | tf_op jit(solution)/shard_map/all_to_all | solution.py:83
  368.8 189.3 %reduce-scatter.2.cloned.1.call-start = ((), (), s32[]{:S(2)}) async-start(), calls=%async_computation.6 | async-start | bytes 2359296 | tf_op jit(solution)/shard_map/reduce_scatter | solution.py:91
Sparse Core Ops, SparseCore 0:
  9.5 33.1 all-gather.2
  44.8 28.5 all-gather.4
  498.6 59.3 reduce-scatter.1
where the time goes:
time: 567 us; the launch traced here: 566 us
  waiting for transfers between devices  338 us (60%)
  blocking collectives  110 us (19%)
  local copies, waits for them, and re-layouts  33.9 us (6%)
  starting transfers between devices  32.5 us (6%)
  matrix products  23.8 us (4%)
  other arithmetic  14.5 us (3%)
  between operations  13.2 us (2%)
    all_to_all x1, waiting for transfers between devices, shards(): lax.all_to_all(send_g, 'tok', split_axis=0, concat_axis=0, tiled=True)  114 us
    all_to_all x1, waiting for transfers between devices, shards(): lax.all_to_all(partial_bf.reshape(n_tok, capacity, full_width), 'tok', sp...  111 us
    all_to_all x1, blocking collectives, shards(): lax.all_to_all(send_x, 'tok', split_axis=0, concat_axis=0, tiled=True)  110 us
    reduce_scatter x1, waiting for transfers between devices, shards(): summed = lax.psum_scatter(combined, 'tp', scatter_dimension=1, tiled=True)  59.6 us
    all_gather x1, waiting for transfers between devices, shards(): lax.all_gather(out_grad, 'tp', axis=1, tiled=True)  31.5 us
    all_gather x1, waiting for transfers between devices, shards(): lax.all_gather(activations, 'tp', axis=1, tiled=True)  20.9 us
    gather x2, local copies, waits for them, and re-layouts, bucket(): jnp.take(rows, token_of, axis=0)  19.8 us
    all_to_all x1, starting transfers between devices, shards(): lax.all_to_all(send_g, 'tok', split_axis=0, concat_axis=0, tiled=True)  16.3 us
  transfers between devices with their start and end apart: 5, of which 5 were waited for; matrix products, arithmetic and copies ran while one was open for 3% of the time, Pallas kernels for 0%

commit v1 on v0

--- a/solution.py
+++ b/solution.py
@@ -1,7 +1,49 @@
+import functools
 import jax
 import jax.numpy as jnp
 from jax import lax
 from jax.sharding import PartitionSpec as P
+
+
+def show_spot(array_in, array_dim):
+    row_out, far_arr, u_next = (
+        lax.axis_size("tp"),
+        lax.axis_index("tp"),
+        array_in.shape[array_dim],
+    )
+    cards = []
+    k = 0
+    while k < row_out:
+        cards.append((k, (k + 1) % row_out))
+        k += 1
+    queue = []
+    k = 0
+    while k < row_out:
+        queue.append((k, (k - 1) % row_out))
+        k += 1
+    f_next = jnp.zeros(
+        (*array_in.shape[:array_dim], row_out * u_next, *array_in.shape[array_dim + 1 :]),
+        array_in.dtype,
+    )
+    f_next = lax.dynamic_update_slice_in_dim(f_next, array_in, far_arr * u_next, axis=array_dim)
+    mixed_arr = last = array_in
+    local_part = row_out // 2
+    jj = 1
+    while jj < local_part + 1:
+        mixed_arr = lax.ppermute(mixed_arr, "tp", cards)
+        f_next = lax.dynamic_update_slice_in_dim(
+            f_next, mixed_arr, (far_arr - jj) % row_out * u_next, axis=array_dim
+        )
+        if jj < row_out - local_part:
+            last = lax.ppermute(last, "tp", queue)
+            f_next = lax.dynamic_update_slice_in_dim(
+                f_next, last, (far_arr + jj) % row_out * u_next, axis=array_dim
+            )
+        jj = jj + 1
+    return f_next
+
+
+supply_the_sections = functools.partial(show_spot, array_dim=1)
 
 
 def routing(routes, n_tok, capacity):
@@ -56,7 +98,7 @@
     contract_last = (((1,), (1,)), ((), ()))
     position, token_of, filled = routing(routes, n_tok, capacity)
     whole_x, whole_g = (
-        lax.all_gather(activations, "tp", axis=1, tiled=True),
+        supply_the_sections(activations),
         lax.all_gather(out_grad, "tp", axis=1, tiled=True),
     )
     width = whole_x.shape[1]

time: 567 us -> 539 us (0.951)
  the two profiles are of different devices: /device:TPU:16 before, /device:TPU:8 now
where the time goes in v1:
time: 539 us; the launch traced here: 538 us
  waiting for transfers between devices  304 us (56%)
  blocking collectives  111 us (21%)
  starting transfers between devices  42.2 us (8%)
  local copies, waits for them, and re-layouts  28.6 us (5%)
  matrix products  23.8 us (4%)
  other arithmetic  14.5 us (3%)
  between operations  13.8 us (3%)
    all_to_all x1, waiting for transfers between devices, shards(): lax.all_to_all(send_g, 'tok', split_axis=0, concat_axis=0, tiled=True)  114 us
    all_to_all x1, waiting for transfers between devices, shards(): lax.all_to_all(partial_bf.reshape(n_tok, capacity, full_width), 'tok', sp...  112 us
    all_to_all x1, blocking collectives, shards(): lax.all_to_all(send_x, 'tok', split_axis=0, concat_axis=0, tiled=True)  111 us
    reduce_scatter x1, waiting for transfers between devices, shards(): summed = lax.psum_scatter(combined, 'tp', scatter_dimension=1, tiled=True)  58.9 us
    all_to_all x1, starting transfers between devices, shards(): lax.all_to_all(partial_bf.reshape(n_tok, capacity, full_width), 'tok', sp...  17.8 us
    all_to_all x1, starting transfers between devices, shards(): lax.all_to_all(send_g, 'tok', split_axis=0, concat_axis=0, tiled=True)  15.3 us
    gather x2, local copies, waits for them, and re-layouts, bucket(): jnp.take(rows, token_of, axis=0)  14.3 us
    gather x2, local copies, waits for them, and re-layouts, combine(): jnp.take(returned, position, axis=0)  12.3 us
  transfers between devices with their start and end apart: 11, of which 7 were waited for; matrix products, arithmetic and copies ran while one was open for 2% of the time, Pallas kernels for 0%

profile of v1, /device:TPU:8, one launch (start us, length us, event | category | flops | bytes accessed | tf_op | source)
XLA Modules:
  0.0 538.1 jit_solution(11801640819723863419)
XLA Ops:
  6.5 0.0 collective-permute-start
  6.6 2.9 collective-permute-start.1
  9.5 0.0 all-gather.2.cloned.1.call-update
  9.5 0.8 copy.23
  10.3 0.1 eq.48
  10.5 0.1 reshape.106
  10.6 0.6 reduce-window.6
  11.2 0.2 slice_reduce_fusion
  11.4 0.1 fusion.43
  11.6 0.1 reduce_sum.41
  11.7 0.1 copy.26
  11.8 0.7 compare_and_fusion.1
  12.5 0.1 convert_reduce_fusion.1
  12.8 0.1 broadcast_in_dim.47
  13.0 0.0 collective-permute-done
  13.0 0.0 collective-permute-start.2
  13.0 0.0 collective-permute-done.1
  13.0 2.9 collective-permute-start.3
  16.0 2.6 collective-permute-done.2
  18.6 0.0 collective-permute-start.4
  18.6 3.0 collective-permute-start.5
  21.6 2.6 collective-permute-done.4
  24.2 0.0 collective-permute-start.6
  24.2 0.0 collective-permute-done.5
  24.3 5.5 %collective-permute-done.6 = bf16[128,512]{1,0:T(8,128)(2,1)S(1)} collective-permute-done((bf16[128,512]{1,0:T(8,128)(2,1)S(1)}, bf16[128,512]{1,0:T(8,128)(2,1)S(1)}, u32[]{:S(2)}, u32[]{:S(2)}) %collective-permute-start.6) | collective-permute-done | bytes 131104 | tf_op jit(solution)/shard_map/ppermute | solution.py:33
  29.8 4.4 gather_fusion.2
  34.2 8.5 %all-gather.2.cloned.1.call-done = bf16[128,4096]{1,0:T(8,128)(2,1)} async-done(((bf16[128,512]{1,0:T(8,128)(2,1)}), bf16[128,4096]{1,0:T(8,128)(2,1)}) %all-gather.2.cloned.1.call-update) | async-done | bytes 1048592 | tf_op jit(solution)/shard_map/all_gather | solution.py:102
  42.8 9.9 %gather_fusion.1 = bf16[512,4096]{1,0:T(8,128)(2,1)} fusion(bf16[128,4096]{1,0:T(8,128)(2,1)} %all-gather.2.cloned.1.call-done, s32[1024]{0:T(1024)S(1)} %pad_clamp_fusion.1), kind=kCustom, calls=%fused_computation.clone | custom fusion | bytes 8390656 | tf_op jit(solution)/shard_map/jit(_take)/gather | solution.py:66
  52.7 5.3 fusion.7
  58.1 111.0 %all_to_all.15 = bf16[64,8,4096]{2,1,0:T(8,128)(2,1)} all-to-all(bf16[64,8,4096]{2,1,0:T(8,128)(2,1)S(1)} %get-tuple-element.12), channel_id=1, replica_groups=mesh['tok'=64,'tp'=8] {'tok'}, dimensions={0} | all-to-all | bytes 8388608 | tf_op jit(solution)/shard_map/all_to_all | solution.py:108
  169.1 15.3 %all-to-all-start = ((bf16[64,8,4096]{2,1,0:T(8,128)(2,1)}), bf16[64,8,4096]{2,1,0:T(8,128)(2,1)}, u32[]{:S(2)}, u32[]{:S(2)}) async-start(bf16[64,8,4096]{2,1,0:T(8,128)(2,1)} %get-tuple-element.13), calls=%async_computation | async-start | bytes 8388608 | tf_op jit(solution)/shard_map/all_to_all | solution.py:109
  184.4 3.7 fusion.1
  188.1 114.1 %all-to-all-done = bf16[64,8,4096]{2,1,0:T(8,128)(2,1)} async-done(((bf16[64,8,4096]{2,1,0:T(8,128)(2,1)}), bf16[64,8,4096]{2,1,0:T(8,128)(2,1)}, u32[]{:S(2)}, u32[]{:S(2)}) %all-to-all-start) | async-done | bytes 4194336 | tf_op jit(solution)/shard_map/all_to_all | solution.py:109
  302.2 5.0 fusion.5
  307.2 8.3 %fusion.10 = f32[512,4096]{1,0:T(8,128)} fusion(bf16[1,192,4096]{2,1,0:T(8,128)(2,1)S(1)} %copy-done.1, f32[512,192]{0,1:T(8,128)} %fusion.5, bf16[1,192,4096]{2,1,0:T(8,128)(2,1)S(1)} %copy-done, bf16[64,8,4096]{2,1,0:T(8,128)(2,1)} %all_to_all.15, f32[512,192]{0,1:T(8,128)S(1)} %fusion.1), kind=kOutput, calls=%fused_computation.19 | convolution fusion | flops 1611595776 | bytes 16515072 | tf_op jit(solution)/shard_map/dot_general | solution.py:121
  315.5 6.8 %fusion = bf16[64,8,4096]{2,1,0:T(8,128)(2,1)} fusion(f32[512,4096]{1,0:T(8,128)} %fusion.10, bf16[1,192,4096]{2,1,0:T(8,128)(2,1)S(1)} %copy-done, f32[512,192]{0,1:T(8,128)} %fusion.5, f32[512,192]{0,1:T(8,128)S(1)} %fusion.1), kind=kOutput, calls=%fused_computation.4 | convolution fusion | flops 810090496 | bytes 14942208 | tf_op jit(solution)/shard_map/dot_general | solution.py:122
  322.3 17.8 %all-to-all-start.2 = ((bf16[64,8,4096]{2,1,0:T(8,128)(2,1)}), bf16[64,8,4096]{2,1,0:T(8,128)(2,1)}, u32[]{:S(2)}, u32[]{:S(2)}) async-start(bf16[64,8,4096]{2,1,0:T(8,128)(2,1)} %fusion), calls=%async_computation.2 | async-start | bytes 8388608 | tf_op jit(solution)/shard_map/all_to_all | solution.py:125
  340.1 0.3 reduce-scatter.2.cloned.1.call-start
  340.4 0.1 copy.27
  340.5 0.1 mul.116
  340.7 111.9 %all-to-all-done.2 = bf16[64,8,4096]{2,1,0:T(8,128)(2,1)} async-done(((bf16[64,8,4096]{2,1,0:T(8,128)(2,1)}), bf16[64,8,4096]{2,1,0:T(8,128)(2,1)}, u32[]{:S(2)}, u32[]{:S(2)}) %all-to-all-start.2) | async-done | bytes 4194336 | tf_op jit(solution)/shard_map/all_to_all | solution.py:125
  452.6 7.9 %gather_fusion = bf16[256,4096]{1,0:T(8,128)(2,1)} fusion(bf16[512,4096]{1,0:T(8,128)(2,1)} %bitcast.10, s32[1024]{0:T(1024)S(1)} %pad_clamp_fusion), kind=kCustom, calls=%fused_computation.2 | custom fusion | bytes 4195328 | tf_op jit(solution)/shard_map/jit(_take)/gather | solution.py:70
  460.5 4.4 gather.10
  464.9 4.0 copy_select_fusion
  468.9 1.8 fusion.9
  470.7 0.0 reduce-scatter.2.cloned.1.call-update
  470.7 58.9 %reduce-scatter.2.cloned.1.call-done = f32[128,512]{1,0:T(8,128)} async-done(((f32[128,4096]{1,0:T(8,128)}), f32[128,512]{1,0:T(8,128)}) %reduce-scatter.2.cloned.1.call-update) | async-done | bytes 262160 | tf_op jit(solution)/shard_map/reduce_scatter | solution.py:133
  529.6 1.6 convert_element_type.45
  (31 shorter events, 0.3 us)
Async XLA Ops:
  6.5 300.7 %copy-start = (bf16[1,192,4096]{2,1,0:T(8,128)(2,1)S(1)}, bf16[1,192,4096]{2,1,0:T(8,128)(2,1)}, u32[]{:S(2)}) copy-start(bf16[1,192,4096]{2,1,0:T(8,128)(2,1)} %param.14) | copy-start | bytes 4718596
  6.5 6.4 %copy-start.2 = (bf16[128,512]{1,0:T(8,128)(2,1)S(1)}, bf16[128,512]{1,0:T(8,128)(2,1)}, u32[]{:S(2)}) copy-start(bf16[128,512]{1,0:T(8,128)(2,1)} %param.9) | copy-start | bytes 393220
  6.5 36.2 %all-gather.2.cloned.1.call-start = ((), (), s32[]{:S(2)}) async-start(), calls=%async_computation.4 | async-start | bytes 1179648 | tf_op jit(solution)/shard_map/all_gather | solution.py:102
  6.5 6.4 %collective-permute-start = (bf16[128,512]{1,0:T(8,128)(2,1)}, bf16[128,512]{1,0:T(8,128)(2,1)S(1)}, u32[]{:S(2)}, u32[]{:S(2)}) collective-permute-start(bf16[128,512]{1,0:T(8,128)(2,1)} %param.9), channel_id=1, source_target_pairs={{0,1},{1,2},{2,3},{3,4},{4,5},{5,6},{6,7},{7,0},{8,9},{9,10},{10,1... | collective-permute-start | bytes 393224 | tf_op jit(solution)/shard_map/ppermute | solution.py:33
  6.6 6.5 %collective-permute-start.1 = (bf16[128,512]{1,0:T(8,128)(2,1)}, bf16[128,512]{1,0:T(8,128)(2,1)S(1)}, u32[]{:S(2)}, u32[]{:S(2)}) collective-permute-start(bf16[128,512]{1,0:T(8,128)(2,1)} %param.9), channel_id=1, source_target_pairs={{0,7},{1,0},{2,1},{3,2},{4,3},{5,4},{6,5},{7,6},{8,15},{9,8},{10,9... | collective-permute-start | bytes 393224 | tf_op jit(solution)/shard_map/ppermute | solution.py:38
  13.0 5.6 %collective-permute-start.2 = (bf16[128,512]{1,0:T(8,128)(2,1)S(1)}, bf16[128,512]{1,0:T(8,128)(2,1)S(1)}, u32[]{:S(2)}, u32[]{:S(2)}) collective-permute-start(bf16[128,512]{1,0:T(8,128)(2,1)S(1)} %collective-permute-done), channel_id=1, source_target_pairs={{0,1},{1,2},{2,3},{3,4},{4,5},{5,6},{6,7},{7,0},{8,9},{9,10},{10,1... | collective-permute-start | bytes 393224 | tf_op jit(solution)/shard_map/ppermute | solution.py:33
  13.0 5.6 %collective-permute-start.3 = (bf16[128,512]{1,0:T(8,128)(2,1)S(1)}, bf16[128,512]{1,0:T(8,128)(2,1)S(1)}, u32[]{:S(2)}, u32[]{:S(2)}) collective-permute-start(bf16[128,512]{1,0:T(8,128)(2,1)S(1)} %collective-permute-done.1), channel_id=1, source_target_pairs={{0,7},{1,0},{2,1},{3,2},{4,3},{5,4},{6,5},{7,6},{8,15},{9,8},{10,9... | collective-permute-start | bytes 393224 | tf_op jit(solution)/shard_map/ppermute | solution.py:38
  18.6 5.6 %collective-permute-start.4 = (bf16[128,512]{1,0:T(8,128)(2,1)S(1)}, bf16[128,512]{1,0:T(8,128)(2,1)S(1)}, u32[]{:S(2)}, u32[]{:S(2)}) collective-permute-start(bf16[128,512]{1,0:T(8,128)(2,1)S(1)} %collective-permute-done.2), channel_id=1, source_target_pairs={{0,1},{1,2},{2,3},{3,4},{4,5},{5,6},{6,7},{7,0},{8,9},{9,10},{10,1... | collective-permute-start | bytes 393224 | tf_op jit(solution)/shard_map/ppermute | solution.py:33
  18.6 5.6 %collective-permute-start.5 = (bf16[128,512]{1,0:T(8,128)(2,1)S(1)}, bf16[128,512]{1,0:T(8,128)(2,1)S(1)}, u32[]{:S(2)}, u32[]{:S(2)}) collective-permute-start(bf16[128,512]{1,0:T(8,128)(2,1)S(1)} %collective-permute-done.3), channel_id=1, source_target_pairs={{0,7},{1,0},{2,1},{3,2},{4,3},{5,4},{6,5},{7,6},{8,15},{9,8},{10,9... | collective-permute-start | bytes 393224 | tf_op jit(solution)/shard_map/ppermute | solution.py:38
  24.2 5.6 %collective-permute-start.6 = (bf16[128,512]{1,0:T(8,128)(2,1)S(1)}, bf16[128,512]{1,0:T(8,128)(2,1)S(1)}, u32[]{:S(2)}, u32[]{:S(2)}) collective-permute-start(bf16[128,512]{1,0:T(8,128)(2,1)S(1)} %collective-permute-done.4), channel_id=1, source_target_pairs={{0,1},{1,2},{2,3},{3,4},{4,5},{5,6},{6,7},{7,0},{8,9},{9,10},{10,1... | collective-permute-start | bytes 393224 | tf_op jit(solution)/shard_map/ppermute | solution.py:33
  169.1 15.3 %copy-start.1 = (bf16[1,192,4096]{2,1,0:T(8,128)(2,1)S(1)}, bf16[1,192,4096]{2,1,0:T(8,128)(2,1)}, u32[]{:S(2)}) copy-start(bf16[1,192,4096]{2,1,0:T(8,128)(2,1)} %param.13) | copy-start | bytes 4718596
  169.1 133.2 %all-to-all-start = ((bf16[64,8,4096]{2,1,0:T(8,128)(2,1)}), bf16[64,8,4096]{2,1,0:T(8,128)(2,1)}, u32[]{:S(2)}, u32[]{:S(2)}) async-start(bf16[64,8,4096]{2,1,0:T(8,128)(2,1)} %get-tuple-element.13), calls=%async_computation | async-start | bytes 8388608 | tf_op jit(solution)/shard_map/all_to_all | solution.py:109
  322.3 18.0 %copy-start.3 = (s32[128,2]{0,1:T(2,128)S(1)}, s32[128,2]{0,1:T(2,128)}, u32[]{:S(2)}) copy-start(s32[128,2]{0,1:T(2,128)} %param.11) | copy-start | bytes 3076
  322.3 18.3 %copy-start.4 = (f32[128,2]{0,1:T(2,128)S(1)}, f32[128,2]{0,1:T(2,128)}, u32[]{:S(2)}) copy-start(f32[128,2]{0,1:T(2,128)} %param.12) | copy-start | bytes 3076
  322.3 130.3 %all-to-all-start.2 = ((bf16[64,8,4096]{2,1,0:T(8,128)(2,1)}), bf16[64,8,4096]{2,1,0:T(8,128)(2,1)}, u32[]{:S(2)}, u32[]{:S(2)}) async-start(bf16[64,8,4096]{2,1,0:T(8,128)(2,1)} %fusion), calls=%async_computation.2 | async-start | bytes 8388608 | tf_op jit(solution)/shard_map/all_to_all | solution.py:125
  340.1 189.6 %reduce-scatter.2.cloned.1.call-start = ((), (), s32[]{:S(2)}) async-start(), calls=%async_computation.5 | async-start | bytes 2359296 | tf_op jit(solution)/shard_map/reduce_scatter | solution.py:133
Sparse Core Ops, SparseCore 0:
  9.6 33.0 all-gather.1
  470.8 58.7 reduce-scatter.1
